TPU v7x, 32 devices: a whole 2x2x4 slice. The times are simulated.
32 devices in a mesh: group: 4 (over y, x), shard: 8 (over z, core).
Axes of the slice: x: 2, y: 2, z: 4, core: 2. Of those that a mesh axis runs over, the one named last changes fastest.
Arguments:
- tokens: bfloat16 [32, 192, 768], P(('group', 'shard')), may hold values from -650 to 650
- norm_gain: float32 [768], replicated, may hold values from 0.1 to 1.9
- w_query: bfloat16 [768, 768], P('shard'), may hold values from -8 to 8
- w_key: bfloat16 [768, 768], P('shard'), may hold values from -0.21875 to 0.21875
- w_value: bfloat16 [768, 768], P('shard'), may hold values from -0.625 to 0.625
- w_out: bfloat16 [768, 768], P('shard'), may hold values from -0.21875 to 0.21875
- owner_map: int32 [4, 8], P('group'), may hold values from 0 to 7, each once within a row
- pair_images: int32 [256, 2], P(('group', 'shard')), may hold values from 0 to 7, as said below
- pair_count: int32 [32], P(('group', 'shard')), may hold values from 1 to 8, 128 in all
- confidence: int32 [256, 2], P(('group', 'shard')), may hold values from 1 to 8
Outputs:
- updated: bfloat16 [32, 192, 768], P(('group', 'shard'))
Inputs may be any that keep to these rules, and one draw needn't show every extreme that they name: `pair_images`: each row names two different images of the listing device's own group, by their index within that group. Device d lists its pairs in its first pair_count[d] rows of pair_images and confidence; the other rows are unused.
All inputs are finite; a program needn't handle non-finite values.
Results may differ from a plain program's by a relative error of at most 0.013.
The roundings to bfloat16 on the way count: a program that leaves them out, or rounds other values in their place, can miss the bound.
Values may be sent and summed in bfloat16 or wider, within the bound.
No kernel may reach another device: no remote copies, remote signals or barrier semaphores. Data moves between devices by JAX's collectives and lax.ppermute only.
A program may use at most 128 MiB of HBM per device.

v0:
```python
import math
import jax
import jax.numpy as jnp
from jax import lax
from jax.sharding import PartitionSpec as P

HEADS = 12
HEAD_DIM = 64


def layer_norm(values, norm_gain):
    values = values.astype(jnp.float32)
    average = jnp.mean(values, axis=-1, keepdims=True)
    centred = values - average
    variance = jnp.mean(centred * centred, axis=-1, keepdims=True)
    return (centred * lax.rsqrt(variance + 1e-05) * norm_gain).astype(jnp.bfloat16)


def attend_many(queries, keys_many, values_many, out_weight):
    count = queries.shape[0]
    length = queries.shape[1]
    query_heads = queries.reshape(count, length, HEADS, HEAD_DIM)
    key_heads = keys_many.reshape(count, length, HEADS, HEAD_DIM)
    value_heads = values_many.reshape(count, length, HEADS, HEAD_DIM)
    scores = jnp.einsum(
        "bqhd,bkhd->bhqk", query_heads, key_heads, preferred_element_type=jnp.float32
    )
    scores = scores * (1.0 / math.sqrt(HEAD_DIM))
    scores = scores - jnp.max(scores, axis=-1, keepdims=True)
    expo = jnp.exp(scores)
    attention = (expo / jnp.sum(expo, axis=-1, keepdims=True)).astype(jnp.bfloat16)
    attended = jnp.einsum(
        "bhqk,bkhd->bqhd", attention, value_heads, preferred_element_type=jnp.float32
    )
    attended = attended.reshape(count * length, HEADS * HEAD_DIM).astype(jnp.bfloat16)
    projected = jnp.dot(attended, out_weight, preferred_element_type=jnp.float32)
    return projected.reshape(count, length, HEADS * HEAD_DIM)


def project_rows(rows, weight):
    return jnp.dot(rows, weight, preferred_element_type=jnp.float32).astype(jnp.bfloat16)


def shards(
    tokens,
    norm_gain,
    w_query,
    w_key,
    w_value,
    w_out,
    owner_map,
    pair_images,
    pair_count,
    confidence,
):
    normed = layer_norm(tokens[0], norm_gain)
    query_weight, key_weight, value_weight, out_weight = (
        lax.all_gather(w_query, "shard", axis=0, tiled=True),
        lax.all_gather(w_key, "shard", axis=0, tiled=True),
        lax.all_gather(w_value, "shard", axis=0, tiled=True),
        lax.all_gather(w_out, "shard", axis=0, tiled=True),
    )
    owners = owner_map[0]
    position = lax.axis_index("shard")
    length = normed.shape[0]
    width = normed.shape[1]
    every_image = lax.all_gather(normed[None], "shard", axis=0, tiled=True)

    def fetch_pair(stored):
        picture = every_image[stored]
        return (project_rows(picture, key_weight), project_rows(picture, value_weight))

    group_pairs, group_conf, group_counts = (
        lax.all_gather(pair_images, "shard", axis=0, tiled=True),
        lax.all_gather(confidence, "shard", axis=0, tiled=True),
        lax.all_gather(pair_count, "shard", axis=0, tiled=True),
    )
    capacity = pair_images.shape[0]
    slot_total = group_pairs.shape[0]
    slot_ids = jnp.arange(slot_total, dtype=jnp.int32)
    usable = slot_ids % capacity < group_counts[slot_ids // capacity]
    store_first = owners[group_pairs[:, 0]]
    store_second = owners[group_pairs[:, 1]]
    querying = jnp.concatenate([store_first, store_second])
    attended_store = jnp.concatenate([store_second, store_first])
    weights_all = jnp.concatenate([group_conf[:, 0], group_conf[:, 1]])
    valid = jnp.concatenate([usable, usable]) & (querying == position)
    direction_ids = jnp.arange(2 * slot_total, dtype=jnp.int32)
    sort_key = jnp.where(valid, direction_ids, 2 * slot_total)
    ordering = jnp.argsort(sort_key)
    chosen_target = attended_store[ordering]
    chosen_weight = weights_all[ordering]
    direction_total = jnp.sum(valid.astype(jnp.int32))
    own_query_rows = project_rows(normed, query_weight)

    def one_direction(number, carried):
        numerator, weight_total = carried
        target_key, target_value = fetch_pair(chosen_target[number])
        projected = attend_many(
            own_query_rows[None], target_key[None], target_value[None], out_weight
        )[0]
        weight_now = chosen_weight[number].astype(jnp.float32)
        return (numerator + weight_now * projected, weight_total + weight_now)

    start = (jnp.zeros((length, width), jnp.float32), jnp.zeros((), jnp.float32))
    numerator, weight_total = lax.fori_loop(0, direction_total, one_direction, start)
    return (numerator / (1.0 + weight_total))[None].astype(jnp.bfloat16)


def solution(mesh):
    in_specs = (
        P(("group", "shard"), None, None),
        P(),
        P("shard", None),
        P("shard", None),
        P("shard", None),
        P("shard", None),
        P("group", None),
        P(("group", "shard"), None),
        P(("group", "shard")),
        P(("group", "shard"), None),
    )
    out_specs = P(("group", "shard"), None, None)
    return jax.shard_map(shards, mesh=mesh, in_specs=in_specs, out_specs=out_specs, check_vma=False)
```

profile of v0, /device:TPU:13, one launch (start us, length us, event | category | flops | bytes accessed | tf_op | source)
XLA Modules:
  0.0 329.1 jit_solution(8869138718722402393)
XLA Ops:
  14.7 6.6 %all-reduce = s32[8]{0:T(128)S(1)} all-reduce(s32[8]{0:T(128)S(1)} %dynamic-update-slice), channel_id=1, replica_groups=mesh['group'=4,'shard'=8] {'shard'}, use_global_device_ids=true, to_apply=%add | all-reduce | flops 8 | bytes 64
  21.3 12.0 %all-gather = s32[8,8,2]{1,2,0:T(2,128)S(1)} all-gather(s32[1,8,2]{1,2,0:T(2,128)S(1)} %bitcast.138), channel_id=1, replica_groups=mesh['group'=4,'shard'=8] {'shard'}, dimensions={0}, use_global_device_ids=true | all-gather | bytes 576 | tf_op jit(solution)/shard_map/all_gather | solution.py:74
  33.4 9.4 %all-gather.1 = s32[8,8,2]{1,2,0:T(2,128)S(1)} all-gather(s32[1,8,2]{1,2,0:T(2,128)S(1)} %bitcast.139), channel_id=1, replica_groups=mesh['group'=4,'shard'=8] {'shard'}, dimensions={0}, use_global_device_ids=true | all-gather | bytes 576 | tf_op jit(solution)/shard_map/all_gather | solution.py:75
  43.6 5.0 %fusion.31 = pred[64]{0:T(512)(128)(4,1)S(1)} fusion(s32[]{:T(128)} %bitcast.13, s32[]{:T(128)} %bitcast.14, s32[]{:T(128)} %bitcast.15, s32[]{:T(128)} %bitcast.16, s32[]{:T(128)} %bitcast.17, s32[]{:T(128)} %bitcast.19, s32[]{:T(128)} %bitcast.18, s32[]{:T(128)} %bitcast.12), kind=kLoop, calls=%fused_computation.74 | loop fusion | flops 2048 | bytes 96 | tf_op jit(solution)/shard_map/lt | solution.py:81
  49.3 5.0 %bitcast_select_fusion.1 = (s32[64]{0:T(128)S(1)}, s32[64]{0:T(128)S(1)}) fusion(s32[64,2]{0,1:T(2,128)S(1)} %reshape.279, s32[]{:T(128)} %bitcast.24, s32[]{:T(128)} %bitcast.25, s32[]{:T(128)} %bitcast.26, s32[]{:T(128)} %bitcast.27, s32[]{:T(128)} %bitcast.28, s32[]{:T(128)} %bitcast.30, s32[]{:T(128)} %bitcast.29, s32[]{:T(128)} %bitcast.23), kind=kLoop, calls=%fused_computation.48 | loop fusion | flops 2176 | bytes 1056 | tf_op jit(solution)/shard_map/gather | solution.py:82
  54.4 2.6 sort.17
  60.2 1.7 convolution_convert_fusion.3
  62.1 19.3 %all-gather.10.cloned.1.call-done = bf16[768,768]{1,0:T(8,128)(2,1)} async-done(((bf16[96,768]{1,0:T(8,128)(2,1)}), bf16[768,768]{1,0:T(8,128)(2,1)}) %all-gather.10.cloned.1.call-update) | async-done | bytes 1179664 | tf_op jit(solution)/shard_map/all_gather | solution.py:60
  81.5 24.0 %all-gather.16.cloned.1.call-done = bf16[768,768]{1,0:T(8,128)(2,1)} async-done(((bf16[96,768]{1,0:T(8,128)(2,1)}), bf16[768,768]{1,0:T(8,128)(2,1)}) %all-gather.16.cloned.1.call-update) | async-done | bytes 1179664 | tf_op jit(solution)/shard_map/all_gather | solution.py:61
  105.4 32.5 %all-gather.8.cloned.1.call-done = bf16[8,192,768]{2,1,0:T(8,128)(2,1)} async-done(((bf16[1,192,768]{2,1,0:T(8,128)(2,1)}), bf16[8,192,768]{2,1,0:T(8,128)(2,1)}) %all-gather.8.cloned.1.call-update) | async-done | bytes 2359312 | tf_op jit(solution)/shard_map/all_gather | solution.py:67
  138.0 183.8 %while.12 = (s32[]{:T(128)}, f32[192,768]{1,0:T(8,128)S(1)}, f32[]{:T(128)}, s32[]{:T(128)}, s32[128]{0:T(128)S(1)}, /*index=5*/s32[128]{0:T(128)S(1)}, bf16[8,1...) while((s32[]{:T(128)}, f32[192,768]{1,0:T(8,128)S(1)}, ...), condition=%wide.region_7.8_spmd, body=%wide.region_4.7_spmd.sunk | while | flops 795672768 | bytes 21547336 | solution.py:106
  142.4 1.9 convolution_convert_fusion.8
  146.0 2.4 fusion.68
  148.4 2.1 convolution_convert_fusion.9
  155.5 1.9 convolution_convert_fusion.8
  157.5 1.4 convolution_convert_fusion.7
  159.1 2.4 fusion.68
  161.5 2.1 convolution_convert_fusion.9
  168.6 1.9 convolution_convert_fusion.8
  170.6 1.4 convolution_convert_fusion.7
  172.2 2.4 fusion.68
  174.6 2.1 convolution_convert_fusion.9
  181.7 1.9 convolution_convert_fusion.8
  183.7 1.4 convolution_convert_fusion.7
  185.3 2.4 fusion.68
  187.7 2.1 convolution_convert_fusion.9
  194.7 1.9 convolution_convert_fusion.8
  196.8 1.4 convolution_convert_fusion.7
  198.4 2.4 fusion.68
  200.7 2.1 convolution_convert_fusion.9
  207.8 1.9 convolution_convert_fusion.8
  209.9 1.4 convolution_convert_fusion.7
  211.4 2.4 fusion.68
  213.8 2.1 convolution_convert_fusion.9
  220.9 1.9 convolution_convert_fusion.8
  223.0 1.4 convolution_convert_fusion.7
  224.5 2.4 fusion.68
  226.9 2.1 convolution_convert_fusion.9
  234.0 1.9 convolution_convert_fusion.8
  236.1 1.4 convolution_convert_fusion.7
  237.6 2.4 fusion.68
  240.0 2.1 convolution_convert_fusion.9
  247.1 1.9 convolution_convert_fusion.8
  249.1 1.4 convolution_convert_fusion.7
  250.7 2.4 fusion.68
  253.1 2.1 convolution_convert_fusion.9
  260.2 1.9 convolution_convert_fusion.8
  262.2 1.4 convolution_convert_fusion.7
  263.8 2.4 fusion.68
  266.2 2.1 convolution_convert_fusion.9
  273.3 1.9 convolution_convert_fusion.8
  275.3 1.4 convolution_convert_fusion.7
  276.9 2.4 fusion.68
  279.3 2.1 convolution_convert_fusion.9
  286.3 1.9 convolution_convert_fusion.8
  288.4 1.4 convolution_convert_fusion.7
  290.0 2.4 fusion.68
  292.3 2.1 convolution_convert_fusion.9
  299.4 1.9 convolution_convert_fusion.8
  303.0 2.4 fusion.68
  305.4 2.1 convolution_convert_fusion.9
  312.5 1.9 convolution_convert_fusion.8
  316.1 2.4 fusion.68
  318.5 2.1 convolution_convert_fusion.9
  (179 shorter events, 45.8 us)
Async XLA Ops:
  6.5 6.8 %copy-start.7 = (u32[32]{0:T(128)S(1)}, u32[32]{0:T(128)}, u32[]{:S(2)}) copy-start(u32[32]{0:T(128)} %constant.98) | copy-start | bytes 388
  6.5 5.2 %copy-start.2 = (bf16[1,192,768]{2,1,0:T(8,128)(2,1)S(1)}, bf16[1,192,768]{2,1,0:T(8,128)(2,1)}, u32[]{:S(2)}) copy-start(bf16[1,192,768]{2,1,0:T(8,128)(2,1)} %param.12) | copy-start | bytes 884740
  6.5 5.2 %copy-start.4 = (f32[768]{0:T(1024)S(1)}, f32[768]{0:T(1024)}, u32[]{:S(2)}) copy-start(f32[768]{0:T(1024)} %param.13) | copy-start | bytes 9220
  6.5 14.8 %copy-start.5 = (s32[8,2]{0,1:T(2,128)S(1)}, s32[8,2]{0,1:T(2,128)}, u32[]{:S(2)}) copy-start(s32[8,2]{0,1:T(2,128)} %param.19) | copy-start | bytes 196
  6.5 26.9 %copy-start.6 = (s32[8,2]{0,1:T(2,128)S(1)}, s32[8,2]{0,1:T(2,128)}, u32[]{:S(2)}) copy-start(s32[8,2]{0,1:T(2,128)} %param.21) | copy-start | bytes 196
  6.5 42.0 %copy-start.3 = (s32[1,8]{1,0:T(1,128)S(1)}, s32[1,8]{1,0:T(1,128)}, u32[]{:S(2)}) copy-start(s32[1,8]{1,0:T(1,128)} %param.18) | copy-start | bytes 100
  6.6 53.7 %all-gather.14.cloned.1.call-start = ((), (), s32[]{:S(2)}) async-start(), calls=%async_computation.3 | async-start | bytes 1327104 | tf_op jit(solution)/shard_map/all_gather | solution.py:58
  7.3 54.8 %all-gather.12.cloned.1.call-start = ((), (), s32[]{:S(2)}) async-start(), calls=%async_computation.2 | async-start | bytes 1327104 | tf_op jit(solution)/shard_map/all_gather | solution.py:59
  8.0 73.4 %all-gather.10.cloned.1.call-start = ((), (), s32[]{:S(2)}) async-start(), calls=%async_computation.1 | async-start | bytes 1327104 | tf_op jit(solution)/shard_map/all_gather | solution.py:60
  8.8 96.6 %all-gather.16.cloned.1.call-start = ((), (), s32[]{:S(2)}) async-start(), calls=%async_computation.4 | async-start | bytes 1327104 | tf_op jit(solution)/shard_map/all_gather | solution.py:61
  9.4 128.6 %all-gather.8.cloned.1.call-start = ((), (), s32[]{:S(2)}) async-start(), calls=%async_computation | async-start | bytes 2654208 | tf_op jit(solution)/shard_map/all_gather | solution.py:67
  142.4 2.1 copy-start
  148.4 2.1 copy-start.1
  155.5 2.1 copy-start
  161.5 2.1 copy-start.1
  168.6 2.1 copy-start
  174.6 2.1 copy-start.1
  181.6 2.1 copy-start
  187.7 2.1 copy-start.1
  194.7 2.1 copy-start
  200.7 2.1 copy-start.1
  207.8 2.1 copy-start
  213.8 2.1 copy-start.1
  220.9 2.1 copy-start
  226.9 2.1 copy-start.1
  234.0 2.1 copy-start
  240.0 2.1 copy-start.1
  247.1 2.1 copy-start
  253.1 2.1 copy-start.1
  260.2 2.1 copy-start
  266.2 2.1 copy-start.1
  273.3 2.1 copy-start
  279.3 2.1 copy-start.1
  286.3 2.1 copy-start
  292.3 2.1 copy-start.1
  299.4 2.1 copy-start
  305.4 2.1 copy-start.1
  312.5 2.1 copy-start
  318.5 2.1 copy-start.1
Sparse Core Ops, SparseCore 0:
  9.0 24.2 all-gather.13
  34.9 22.3 all-gather.11
  59.0 22.4 all-gather.9
  83.0 22.4 all-gather.15
  106.9 30.9 all-gather.7
where the time goes:
time: 331 us; the launch traced here: 329 us
  matrix products  117 us (35%)
  waiting for transfers between devices  78.4 us (24%)
  loops' own time  47 us (14%)
  blocking collectives  28 us (8%)
  local copies, waits for them, and re-layouts  26.9 us (8%)
  other arithmetic  17.4 us (5%)
  between operations  13.9 us (4%)
    dot_general x29, matrix products, project_rows(): jnp.dot(rows, weight, preferred_element_type=jnp.float32)  47 us
    another operation x1, loops' own time, shards(): lax.fori_loop(0, direction_total, one_direction, start)  47 us
    sub x14, matrix products, attend_many(): scores = scores - jnp.max(scores, axis=-1, keepdims=True)  33.4 us
    all_gather x1, waiting for transfers between devices, shards(): every_image = lax.all_gather(normed[None], 'shard', axis=0, tiled=True)  32.5 us
    dot_general x14, matrix products, attend_many(): jnp.einsum('bhqk,bkhd->bqhd', attention, value_heads, preferred_element_t...  29.7 us
    all_gather x1, waiting for transfers between devices, shards(): lax.all_gather(w_out, 'shard', axis=0, tiled=True)  24 us
    all_gather x1, waiting for transfers between devices, shards(): lax.all_gather(w_value, 'shard', axis=0, tiled=True)  19.3 us
    all_gather x1, blocking collectives, shards(): lax.all_gather(pair_images, 'shard', axis=0, tiled=True)  12 us
  transfers between devices with their start and end apart: 5, of which 3 were waited for; matrix products, arithmetic and copies ran while one was open for 7% of the time, Pallas kernels for 0%

commit v1 on v0

--- a/solution.py
+++ b/solution.py
@@ -6,6 +6,21 @@
 
 HEADS = 12
 HEAD_DIM = 64
+
+
+def _lay_columns(state, link_axis):
+    crops = [state]
+    no = 0
+    nd = lax.axis_size(link_axis)
+    while no < nd - 1:
+        newest = lax.ppermute(
+            crops[-1], axis_name=link_axis, perm=[(kk, (kk + 1) % nd) for kk in range(nd)]
+        )
+        crops.append(newest)
+        no += 1
+    near = jnp.concatenate(crops[::-1], axis=0)
+    piece_now = lax.axis_index(link_axis)
+    return jnp.roll(near, (piece_now + 1) * state.shape[0], axis=0)
 
 
 def layer_norm(values, norm_gain):
@@ -64,7 +79,7 @@
     position = lax.axis_index("shard")
     length = normed.shape[0]
     width = normed.shape[1]
-    every_image = lax.all_gather(normed[None], "shard", axis=0, tiled=True)
+    every_image = _lay_columns(normed[None], "shard")
 
     def fetch_pair(stored):
         picture = every_image[stored]

time: 331 us -> 300 us (0.906)
  waiting for transfers between devices: 78.4 us -> 33.4 us
  starting transfers between devices: 0.19 us -> 10.7 us
  local copies, waits for them, and re-layouts: 26.9 us -> 31.1 us
  loops' own time: 47 us -> 43.3 us
  blocking collectives: 28 us -> 31.6 us
    all_gather x1 -> x0, waiting for transfers between devices: 32.5 us -> none  [shards(): every_image = lax.all_gather(normed[None], 'shard', axis=0, tiled=True)]
    all_gather x1, waiting for transfers between devices: 24 us -> 0.01 us  [shards(): lax.all_gather(w_out, 'shard', axis=0, tiled=True)]
    all_gather x1, waiting for transfers between devices: 19.3 us -> 0.01 us  [shards(): lax.all_gather(w_value, 'shard', axis=0, tiled=True)]
    ppermute x0 -> x7, waiting for transfers between devices: none -> 16.9 us  [_lay_columns(): lax.ppermute(crops[-1], axis_name=link_axis, perm=[(kk, (kk + 1) % nd) fo...]
    all_gather x1, waiting for transfers between devices: 0.02 us -> 14.4 us  [shards(): lax.all_gather(w_key, 'shard', axis=0, tiled=True)]
    ppermute x0 -> x7, starting transfers between devices: none -> 10.6 us  [_lay_columns(): lax.ppermute(crops[-1], axis_name=link_axis, perm=[(kk, (kk + 1) % nd) fo...]
    unnamed x1, blocking collectives: 6.63 us -> 12.3 us
    all_gather x1, blocking collectives: 12 us -> 8.08 us  [shards(): lax.all_gather(pair_images, 'shard', axis=0, tiled=True)]
  transfers between devices with their start and end apart: 5 -> 11, of which waited for: 3 -> 4; matrix products, arithmetic and copies ran while one was open for 7% -> 9% of each run, Pallas kernels for 0% -> 0%
where the time goes in v1:
time: 300 us; the launch traced here: 298 us
  matrix products  116 us (39%)
  loops' own time  43.3 us (14%)
  waiting for transfers between devices  33.4 us (11%)
  blocking collectives  31.6 us (11%)
  local copies, waits for them, and re-layouts  31.1 us (10%)
  other arithmetic  18.2 us (6%)
  between operations  14.1 us (5%)
  starting transfers between devices  10.7 us (4%)
    dot_general x29, matrix products, project_rows(): jnp.dot(rows, weight, preferred_element_type=jnp.float32)  45.8 us
    another operation x1, loops' own time, shards(): lax.fori_loop(0, direction_total, one_direction, start)  43.3 us
    sub x14, matrix products, attend_many(): scores = scores - jnp.max(scores, axis=-1, keepdims=True)  33.3 us
    dot_general x14, matrix products, attend_many(): jnp.einsum('bhqk,bkhd->bqhd', attention, value_heads, preferred_element_t...  29.7 us
    ppermute x7, waiting for transfers between devices, _lay_columns(): lax.ppermute(crops[-1], axis_name=link_axis, perm=[(kk, (kk + 1) % nd) fo...  16.9 us
    all_gather x1, waiting for transfers between devices, shards(): lax.all_gather(w_key, 'shard', axis=0, tiled=True)  14.4 us
    unnamed x1, blocking collectives  12.3 us
    all_gather x1, blocking collectives, shards(): lax.all_gather(confidence, 'shard', axis=0, tiled=True)  11.1 us
  transfers between devices with their start and end apart: 11, of which 4 were waited for; matrix products, arithmetic and copies ran while one was open for 9% of the time, Pallas kernels for 0%

profile of v1, /device:TPU:13, one launch (start us, length us, event | category | flops | bytes accessed | tf_op | source)
XLA Modules:
  0.0 298.4 jit_solution(1808169786943829121)
XLA Ops:
  12.3 1.9 collective-permute-start
  14.2 3.7 %collective-permute-done = bf16[1,192,768]{2,1,0:T(8,128)(2,1)S(1)} collective-permute-done((bf16[1,192,768]{2,1,0:T(8,128)(2,1)S(1)}, bf16[1,192,768]{2,1,0:T(8,128)(2,1)S(1)}, u32[]{:S(2)}, u32[]{:S(2)}) %collective-permute-start) | collective-permute-done | bytes 294944 | tf_op jit(solution)/shard_map/ppermute | solution.py:16
  17.9 2.5 collective-permute-start.1
  23.1 12.3 %all-reduce = s32[8]{0:T(128)S(1)} all-reduce(s32[8]{0:T(128)S(1)} %dynamic-update-slice), channel_id=1, replica_groups=mesh['group'=4,'shard'=8] {'shard'}, use_global_device_ids=true, to_apply=%add | all-reduce | flops 8 | bytes 64
  35.4 8.1 %all-gather = s32[8,8,2]{1,2,0:T(2,128)S(1)} all-gather(s32[1,8,2]{1,2,0:T(2,128)} %bitcast.138), channel_id=1, replica_groups=mesh['group'=4,'shard'=8] {'shard'}, dimensions={0}, use_global_device_ids=true | all-gather | bytes 576 | tf_op jit(solution)/shard_map/all_gather | solution.py:89
  43.6 11.1 %all-gather.1 = s32[8,8,2]{1,2,0:T(2,128)S(1)} all-gather(s32[1,8,2]{1,2,0:T(2,128)} %bitcast.139), channel_id=1, replica_groups=mesh['group'=4,'shard'=8] {'shard'}, dimensions={0}, use_global_device_ids=true | all-gather | bytes 576 | tf_op jit(solution)/shard_map/all_gather | solution.py:90
  55.5 5.1 %fusion.31 = pred[64]{0:T(512)(128)(4,1)S(1)} fusion(s32[]{:T(128)} %bitcast.13, s32[]{:T(128)} %bitcast.14, s32[]{:T(128)} %bitcast.15, s32[]{:T(128)} %bitcast.16, s32[]{:T(128)} %bitcast.17, s32[]{:T(128)} %bitcast.19, s32[]{:T(128)} %bitcast.18, s32[]{:T(128)} %bitcast.12), kind=kLoop, calls=%fused_computation.90 | loop fusion | flops 2048 | bytes 96 | tf_op jit(solution)/shard_map/lt | solution.py:96
  60.6 1.6 fusion.37
  62.3 5.1 %bitcast_select_fusion.1 = (s32[64]{0:T(128)S(1)}, s32[64]{0:T(128)S(1)}) fusion(s32[64,2]{0,1:T(2,128)S(1)} %reshape.279, s32[]{:T(128)} %bitcast.24, s32[]{:T(128)} %bitcast.25, s32[]{:T(128)} %bitcast.26, s32[]{:T(128)} %bitcast.27, s32[]{:T(128)} %bitcast.28, s32[]{:T(128)} %bitcast.30, s32[]{:T(128)} %bitcast.29, s32[]{:T(128)} %bitcast.23), kind=kLoop, calls=%fused_computation.64 | loop fusion | flops 2176 | bytes 1056 | tf_op jit(solution)/shard_map/gather | solution.py:97
  67.5 2.5 sort.17
  71.1 10.2 %collective-permute-done.4 = bf16[1,192,768]{2,1,0:T(8,128)(2,1)S(1)} collective-permute-done((bf16[1,192,768]{2,1,0:T(8,128)(2,1)S(1)}, bf16[1,192,768]{2,1,0:T(8,128)(2,1)S(1)}, u32[]{:S(2)}, u32[]{:S(2)}) %collective-permute-start.4) | collective-permute-done | bytes 294944 | tf_op jit(solution)/shard_map/ppermute | solution.py:16
  81.3 2.6 collective-permute-start.5
  84.6 3.0 %collective-permute-done.5 = bf16[1,192,768]{2,1,0:T(8,128)(2,1)S(1)} collective-permute-done((bf16[1,192,768]{2,1,0:T(8,128)(2,1)S(1)}, bf16[1,192,768]{2,1,0:T(8,128)(2,1)S(1)}, u32[]{:S(2)}, u32[]{:S(2)}) %collective-permute-start.5) | collective-permute-done | bytes 294944 | tf_op jit(solution)/shard_map/ppermute | solution.py:16
  87.6 2.5 collective-permute-start.6
  92.7 1.9 convolution_convert_fusion.3
  95.6 1.6 constant_dynamic-slice_fusion
  97.2 14.4 %all-gather.9.cloned.1.call-done = bf16[768,768]{1,0:T(8,128)(2,1)} async-done(((bf16[96,768]{1,0:T(8,128)(2,1)}), bf16[768,768]{1,0:T(8,128)(2,1)}) %all-gather.9.cloned.1.call-update) | async-done | bytes 1179664 | tf_op jit(solution)/shard_map/all_gather | solution.py:74
  111.6 179.5 %while.12 = (s32[]{:T(128)}, f32[192,768]{1,0:T(8,128)S(1)}, f32[]{:T(128)}, s32[]{:T(128)}, s32[128]{0:T(128)S(1)}, /*index=5*/s32[128]{0:T(128)S(1)}, bf16[8,1...) while((s32[]{:T(128)}, f32[192,768]{1,0:T(8,128)S(1)}, ...), condition=%wide.region_7.8_spmd, body=%wide.region_4.7_spmd.sunk | while | flops 795672768 | bytes 21547328 | solution.py:121
  114.6 1.8 convolution_convert_fusion.8
  116.5 2.4 fusion.68
  120.5 2.1 convolution_convert_fusion.9
  127.3 1.8 convolution_convert_fusion.8
  129.3 2.4 fusion.68
  131.7 1.4 convolution_convert_fusion.7
  133.2 2.1 convolution_convert_fusion.9
  140.1 1.8 convolution_convert_fusion.8
  142.1 2.4 fusion.68
  144.5 1.4 convolution_convert_fusion.7
  146.0 2.1 convolution_convert_fusion.9
  152.9 1.8 convolution_convert_fusion.8
  154.8 2.4 fusion.68
  157.2 1.4 convolution_convert_fusion.7
  158.8 2.1 convolution_convert_fusion.9
  165.7 1.8 convolution_convert_fusion.8
  167.6 2.4 fusion.68
  170.0 1.4 convolution_convert_fusion.7
  171.6 2.1 convolution_convert_fusion.9
  178.4 1.8 convolution_convert_fusion.8
  180.4 2.4 fusion.68
  184.3 2.1 convolution_convert_fusion.9
  191.2 1.8 convolution_convert_fusion.8
  193.2 2.4 fusion.68
  197.1 2.1 convolution_convert_fusion.9
  204.0 1.8 convolution_convert_fusion.8
  205.9 2.4 fusion.68
  209.9 2.1 convolution_convert_fusion.9
  216.8 1.8 convolution_convert_fusion.8
  218.7 2.4 fusion.68
  222.7 2.1 convolution_convert_fusion.9
  229.5 1.8 convolution_convert_fusion.8
  231.5 2.4 fusion.68
  235.4 2.1 convolution_convert_fusion.9
  242.3 1.8 convolution_convert_fusion.8
  244.3 2.4 fusion.68
  248.2 2.1 convolution_convert_fusion.9
  255.1 1.8 convolution_convert_fusion.8
  257.0 2.4 fusion.68
  261.0 2.1 convolution_convert_fusion.9
  267.9 1.8 convolution_convert_fusion.8
  269.8 2.4 fusion.68
  273.8 2.1 convolution_convert_fusion.9
  280.6 1.8 convolution_convert_fusion.8
  282.6 2.4 fusion.68
  286.5 2.1 convolution_convert_fusion.9
  (199 shorter events, 57.5 us)
Async XLA Ops:
  6.5 86.1 %all-gather.11.cloned.1.call-start = ((), (), s32[]{:S(2)}) async-start(), calls=%async_computation.2 | async-start | bytes 1327104 | tf_op jit(solution)/shard_map/all_gather | solution.py:73
  7.3 89.9 %all-gather.13.cloned.1.call-start = ((), (), s32[]{:S(2)}) async-start(), calls=%async_computation.3 | async-start | bytes 1327104 | tf_op jit(solution)/shard_map/all_gather | solution.py:76
  8.0 89.2 %all-gather.7.cloned.1.call-start = ((), (), s32[]{:S(2)}) async-start(), calls=%async_computation | async-start | bytes 1327104 | tf_op jit(solution)/shard_map/all_gather | solution.py:75
  8.7 86.2 %copy-start.2 = (bf16[1,192,768]{2,1,0:T(8,128)(2,1)S(1)}, bf16[1,192,768]{2,1,0:T(8,128)(2,1)}, u32[]{:S(2)}) copy-start(bf16[1,192,768]{2,1,0:T(8,128)(2,1)} %param.12) | copy-start | bytes 884740
  8.8 86.2 %copy-start.3 = (f32[768]{0:T(1024)S(1)}, f32[768]{0:T(1024)}, u32[]{:S(2)}) copy-start(f32[768]{0:T(1024)} %param.13) | copy-start | bytes 9220
  8.8 102.8 %all-gather.9.cloned.1.call-start = ((), (), s32[]{:S(2)}) async-start(), calls=%async_computation.1 | async-start | bytes 1327104 | tf_op jit(solution)/shard_map/all_gather | solution.py:74
  12.3 5.6 %collective-permute-start = (bf16[1,192,768]{2,1,0:T(8,128)(2,1)S(1)}, bf16[1,192,768]{2,1,0:T(8,128)(2,1)S(1)}, u32[]{:S(2)}, u32[]{:S(2)}) collective-permute-start(bf16[1,192,768]{2,1,0:T(8,128)(2,1)S(1)} %fusion.19), channel_id=1, source_target_pairs={{0,1},{1,2},{2,3},{3,4},{4,5},{5,6},{6,7},{7,0},{8,9},{9,10},{10,1... | collective-permute-start | bytes 884744 | tf_op jit(solution)/shard_map/ppermute | solution.py:16
  17.9 36.9 %collective-permute-start.1 = (bf16[1,192,768]{2,1,0:T(8,128)(2,1)S(1)}, bf16[1,192,768]{2,1,0:T(8,128)(2,1)S(1)}, u32[]{:S(2)}, u32[]{:S(2)}) collective-permute-start(bf16[1,192,768]{2,1,0:T(8,128)(2,1)S(1)} %collective-permute-done), channel_id=1, source_target_pairs={{0,1},{1,2},{2,3},{3,4},{4,5},{5,6},{6,7},{7,0},{8,9},{9,10},{10,1... | collective-permute-start | bytes 884744 | tf_op jit(solution)/shard_map/ppermute | solution.py:16
  54.8 7.5 %collective-permute-start.2 = (bf16[1,192,768]{2,1,0:T(8,128)(2,1)S(1)}, bf16[1,192,768]{2,1,0:T(8,128)(2,1)S(1)}, u32[]{:S(2)}, u32[]{:S(2)}) collective-permute-start(bf16[1,192,768]{2,1,0:T(8,128)(2,1)S(1)} %collective-permute-done.1), channel_id=1, source_target_pairs={{0,1},{1,2},{2,3},{3,4},{4,5},{5,6},{6,7},{7,0},{8,9},{9,10},{10,1... | collective-permute-start | bytes 884744 | tf_op jit(solution)/shard_map/ppermute | solution.py:16
  62.3 7.8 %collective-permute-start.3 = (bf16[1,192,768]{2,1,0:T(8,128)(2,1)S(1)}, bf16[1,192,768]{2,1,0:T(8,128)(2,1)S(1)}, u32[]{:S(2)}, u32[]{:S(2)}) collective-permute-start(bf16[1,192,768]{2,1,0:T(8,128)(2,1)S(1)} %collective-permute-done.2), channel_id=1, source_target_pairs={{0,1},{1,2},{2,3},{3,4},{4,5},{5,6},{6,7},{7,0},{8,9},{9,10},{10,1... | collective-permute-start | bytes 884744 | tf_op jit(solution)/shard_map/ppermute | solution.py:16
  70.1 11.3 %collective-permute-start.4 = (bf16[1,192,768]{2,1,0:T(8,128)(2,1)S(1)}, bf16[1,192,768]{2,1,0:T(8,128)(2,1)S(1)}, u32[]{:S(2)}, u32[]{:S(2)}) collective-permute-start(bf16[1,192,768]{2,1,0:T(8,128)(2,1)S(1)} %collective-permute-done.3), channel_id=1, source_target_pairs={{0,1},{1,2},{2,3},{3,4},{4,5},{5,6},{6,7},{7,0},{8,9},{9,10},{10,1... | collective-permute-start | bytes 884744 | tf_op jit(solution)/shard_map/ppermute | solution.py:16
  81.3 6.3 %collective-permute-start.5 = (bf16[1,192,768]{2,1,0:T(8,128)(2,1)S(1)}, bf16[1,192,768]{2,1,0:T(8,128)(2,1)S(1)}, u32[]{:S(2)}, u32[]{:S(2)}) collective-permute-start(bf16[1,192,768]{2,1,0:T(8,128)(2,1)S(1)} %collective-permute-done.4), channel_id=1, source_target_pairs={{0,1},{1,2},{2,3},{3,4},{4,5},{5,6},{6,7},{7,0},{8,9},{9,10},{10,1... | collective-permute-start | bytes 884744 | tf_op jit(solution)/shard_map/ppermute | solution.py:16
  87.6 7.1 %collective-permute-start.6 = (bf16[1,192,768]{2,1,0:T(8,128)(2,1)S(1)}, bf16[1,192,768]{2,1,0:T(8,128)(2,1)S(1)}, u32[]{:S(2)}, u32[]{:S(2)}) collective-permute-start(bf16[1,192,768]{2,1,0:T(8,128)(2,1)S(1)} %collective-permute-done.5), channel_id=1, source_target_pairs={{0,1},{1,2},{2,3},{3,4},{4,5},{5,6},{6,7},{7,0},{8,9},{9,10},{10,1... | collective-permute-start | bytes 884744 | tf_op jit(solution)/shard_map/ppermute | solution.py:16
  112.3 6.6 %copy-start.1 = (bf16[768,768]{1,0:T(8,128)(2,1)S(1)}, bf16[768,768]{1,0:T(8,128)(2,1)}, u32[]{:S(2)}) copy-start(bf16[768,768]{1,0:T(8,128)(2,1)} %get-tuple-element.257) | copy-start | bytes 3538948 | tf_op jit(solution)/shard_map/while
  120.3 3.6 %copy-start = (bf16[768,768]{1,0:T(8,128)(2,1)S(1)}, bf16[768,768]{1,0:T(8,128)(2,1)}, u32[]{:S(2)}) copy-start(bf16[768,768]{1,0:T(8,128)(2,1)} %get-tuple-element.260) | copy-start | bytes 3538948 | tf_op jit(solution)/shard_map/while
  125.0 6.6 %copy-start.1 = (bf16[768,768]{1,0:T(8,128)(2,1)S(1)}, bf16[768,768]{1,0:T(8,128)(2,1)}, u32[]{:S(2)}) copy-start(bf16[768,768]{1,0:T(8,128)(2,1)} %get-tuple-element.257) | copy-start | bytes 3538948 | tf_op jit(solution)/shard_map/while
  133.0 3.6 %copy-start = (bf16[768,768]{1,0:T(8,128)(2,1)S(1)}, bf16[768,768]{1,0:T(8,128)(2,1)}, u32[]{:S(2)}) copy-start(bf16[768,768]{1,0:T(8,128)(2,1)} %get-tuple-element.260) | copy-start | bytes 3538948 | tf_op jit(solution)/shard_map/while
  137.8 6.6 %copy-start.1 = (bf16[768,768]{1,0:T(8,128)(2,1)S(1)}, bf16[768,768]{1,0:T(8,128)(2,1)}, u32[]{:S(2)}) copy-start(bf16[768,768]{1,0:T(8,128)(2,1)} %get-tuple-element.257) | copy-start | bytes 3538948 | tf_op jit(solution)/shard_map/while
  145.8 3.6 %copy-start = (bf16[768,768]{1,0:T(8,128)(2,1)S(1)}, bf16[768,768]{1,0:T(8,128)(2,1)}, u32[]{:S(2)}) copy-start(bf16[768,768]{1,0:T(8,128)(2,1)} %get-tuple-element.260) | copy-start | bytes 3538948 | tf_op jit(solution)/shard_map/while
  150.6 6.6 %copy-start.1 = (bf16[768,768]{1,0:T(8,128)(2,1)S(1)}, bf16[768,768]{1,0:T(8,128)(2,1)}, u32[]{:S(2)}) copy-start(bf16[768,768]{1,0:T(8,128)(2,1)} %get-tuple-element.257) | copy-start | bytes 3538948 | tf_op jit(solution)/shard_map/while
  158.6 3.6 %copy-start = (bf16[768,768]{1,0:T(8,128)(2,1)S(1)}, bf16[768,768]{1,0:T(8,128)(2,1)}, u32[]{:S(2)}) copy-start(bf16[768,768]{1,0:T(8,128)(2,1)} %get-tuple-element.260) | copy-start | bytes 3538948 | tf_op jit(solution)/shard_map/while
  163.4 6.6 %copy-start.1 = (bf16[768,768]{1,0:T(8,128)(2,1)S(1)}, bf16[768,768]{1,0:T(8,128)(2,1)}, u32[]{:S(2)}) copy-start(bf16[768,768]{1,0:T(8,128)(2,1)} %get-tuple-element.257) | copy-start | bytes 3538948 | tf_op jit(solution)/shard_map/while
  171.4 3.6 %copy-start = (bf16[768,768]{1,0:T(8,128)(2,1)S(1)}, bf16[768,768]{1,0:T(8,128)(2,1)}, u32[]{:S(2)}) copy-start(bf16[768,768]{1,0:T(8,128)(2,1)} %get-tuple-element.260) | copy-start | bytes 3538948 | tf_op jit(solution)/shard_map/while
  176.1 6.6 %copy-start.1 = (bf16[768,768]{1,0:T(8,128)(2,1)S(1)}, bf16[768,768]{1,0:T(8,128)(2,1)}, u32[]{:S(2)}) copy-start(bf16[768,768]{1,0:T(8,128)(2,1)} %get-tuple-element.257) | copy-start | bytes 3538948 | tf_op jit(solution)/shard_map/while
  184.1 3.6 %copy-start = (bf16[768,768]{1,0:T(8,128)(2,1)S(1)}, bf16[768,768]{1,0:T(8,128)(2,1)}, u32[]{:S(2)}) copy-start(bf16[768,768]{1,0:T(8,128)(2,1)} %get-tuple-element.260) | copy-start | bytes 3538948 | tf_op jit(solution)/shard_map/while
  188.9 6.6 %copy-start.1 = (bf16[768,768]{1,0:T(8,128)(2,1)S(1)}, bf16[768,768]{1,0:T(8,128)(2,1)}, u32[]{:S(2)}) copy-start(bf16[768,768]{1,0:T(8,128)(2,1)} %get-tuple-element.257) | copy-start | bytes 3538948 | tf_op jit(solution)/shard_map/while
  196.9 3.6 %copy-start = (bf16[768,768]{1,0:T(8,128)(2,1)S(1)}, bf16[768,768]{1,0:T(8,128)(2,1)}, u32[]{:S(2)}) copy-start(bf16[768,768]{1,0:T(8,128)(2,1)} %get-tuple-element.260) | copy-start | bytes 3538948 | tf_op jit(solution)/shard_map/while
  201.7 6.6 %copy-start.1 = (bf16[768,768]{1,0:T(8,128)(2,1)S(1)}, bf16[768,768]{1,0:T(8,128)(2,1)}, u32[]{:S(2)}) copy-start(bf16[768,768]{1,0:T(8,128)(2,1)} %get-tuple-element.257) | copy-start | bytes 3538948 | tf_op jit(solution)/shard_map/while
  209.7 3.6 %copy-start = (bf16[768,768]{1,0:T(8,128)(2,1)S(1)}, bf16[768,768]{1,0:T(8,128)(2,1)}, u32[]{:S(2)}) copy-start(bf16[768,768]{1,0:T(8,128)(2,1)} %get-tuple-element.260) | copy-start | bytes 3538948 | tf_op jit(solution)/shard_map/while
  214.5 6.6 %copy-start.1 = (bf16[768,768]{1,0:T(8,128)(2,1)S(1)}, bf16[768,768]{1,0:T(8,128)(2,1)}, u32[]{:S(2)}) copy-start(bf16[768,768]{1,0:T(8,128)(2,1)} %get-tuple-element.257) | copy-start | bytes 3538948 | tf_op jit(solution)/shard_map/while
  222.5 3.6 %copy-start = (bf16[768,768]{1,0:T(8,128)(2,1)S(1)}, bf16[768,768]{1,0:T(8,128)(2,1)}, u32[]{:S(2)}) copy-start(bf16[768,768]{1,0:T(8,128)(2,1)} %get-tuple-element.260) | copy-start | bytes 3538948 | tf_op jit(solution)/shard_map/while
  227.2 6.6 %copy-start.1 = (bf16[768,768]{1,0:T(8,128)(2,1)S(1)}, bf16[768,768]{1,0:T(8,128)(2,1)}, u32[]{:S(2)}) copy-start(bf16[768,768]{1,0:T(8,128)(2,1)} %get-tuple-element.257) | copy-start | bytes 3538948 | tf_op jit(solution)/shard_map/while
  235.2 3.6 %copy-start = (bf16[768,768]{1,0:T(8,128)(2,1)S(1)}, bf16[768,768]{1,0:T(8,128)(2,1)}, u32[]{:S(2)}) copy-start(bf16[768,768]{1,0:T(8,128)(2,1)} %get-tuple-element.260) | copy-start | bytes 3538948 | tf_op jit(solution)/shard_map/while
  240.0 6.6 %copy-start.1 = (bf16[768,768]{1,0:T(8,128)(2,1)S(1)}, bf16[768,768]{1,0:T(8,128)(2,1)}, u32[]{:S(2)}) copy-start(bf16[768,768]{1,0:T(8,128)(2,1)} %get-tuple-element.257) | copy-start | bytes 3538948 | tf_op jit(solution)/shard_map/while
  248.0 3.6 %copy-start = (bf16[768,768]{1,0:T(8,128)(2,1)S(1)}, bf16[768,768]{1,0:T(8,128)(2,1)}, u32[]{:S(2)}) copy-start(bf16[768,768]{1,0:T(8,128)(2,1)} %get-tuple-element.260) | copy-start | bytes 3538948 | tf_op jit(solution)/shard_map/while
  252.8 6.6 %copy-start.1 = (bf16[768,768]{1,0:T(8,128)(2,1)S(1)}, bf16[768,768]{1,0:T(8,128)(2,1)}, u32[]{:S(2)}) copy-start(bf16[768,768]{1,0:T(8,128)(2,1)} %get-tuple-element.257) | copy-start | bytes 3538948 | tf_op jit(solution)/shard_map/while
  260.8 3.6 %copy-start = (bf16[768,768]{1,0:T(8,128)(2,1)S(1)}, bf16[768,768]{1,0:T(8,128)(2,1)}, u32[]{:S(2)}) copy-start(bf16[768,768]{1,0:T(8,128)(2,1)} %get-tuple-element.260) | copy-start | bytes 3538948 | tf_op jit(solution)/shard_map/while
  265.6 6.6 %copy-start.1 = (bf16[768,768]{1,0:T(8,128)(2,1)S(1)}, bf16[768,768]{1,0:T(8,128)(2,1)}, u32[]{:S(2)}) copy-start(bf16[768,768]{1,0:T(8,128)(2,1)} %get-tuple-element.257) | copy-start | bytes 3538948 | tf_op jit(solution)/shard_map/while
  273.6 3.6 %copy-start = (bf16[768,768]{1,0:T(8,128)(2,1)S(1)}, bf16[768,768]{1,0:T(8,128)(2,1)}, u32[]{:S(2)}) copy-start(bf16[768,768]{1,0:T(8,128)(2,1)} %get-tuple-element.260) | copy-start | bytes 3538948 | tf_op jit(solution)/shard_map/while
  278.3 6.6 %copy-start.1 = (bf16[768,768]{1,0:T(8,128)(2,1)S(1)}, bf16[768,768]{1,0:T(8,128)(2,1)}, u32[]{:S(2)}) copy-start(bf16[768,768]{1,0:T(8,128)(2,1)} %get-tuple-element.257) | copy-start | bytes 3538948 | tf_op jit(solution)/shard_map/while
  286.3 3.6 %copy-start = (bf16[768,768]{1,0:T(8,128)(2,1)S(1)}, bf16[768,768]{1,0:T(8,128)(2,1)}, u32[]{:S(2)}) copy-start(bf16[768,768]{1,0:T(8,128)(2,1)} %get-tuple-element.260) | copy-start | bytes 3538948 | tf_op jit(solution)/shard_map/while
Sparse Core Ops, SparseCore 0:
  9.0 26.5 all-gather.10
  37.2 22.2 all-gather.12
  61.2 24.5 all-gather.6
  87.3 24.2 all-gather.8
